TPU v7x, 32 devices: a whole 2x2x4 slice. The times are simulated.
32 devices in a mesh: dp: 16 (over z, x, core), head: 2 (over y).
Axes of the slice: x: 2, y: 2, z: 4, core: 2. Of those that a mesh axis runs over, the one named last changes fastest.
Arguments:
- tokens: bfloat16 [4, 8192, 768], P(None, 'dp'), may hold values from -6 to 6
- live: int32 [4, 8192], P(None, 'dp'), may hold values from 0 to 1, as said below
- bucket: int32 [4], replicated, may hold values from 64 to 512, as said below
- query_weight: bfloat16 [768, 768], P('dp', 'head'), may hold values from -0.21875 to 0.21875
- key_weight: bfloat16 [768, 768], P('dp', 'head'), may hold values from -0.21875 to 0.21875
- value_weight: bfloat16 [768, 768], P('dp', 'head'), may hold values from -0.21875 to 0.21875
- output_weight: bfloat16 [768, 768], P('head', 'dp'), may hold values from -0.875 to 0.875
- inner_weight: bfloat16 [768, 3072], P('dp', 'head'), may hold values from -0.21875 to 0.21875
- outer_weight: bfloat16 [3072, 768], P('head', 'dp'), may hold values from -0.109375 to 0.109375
- query_bias_vector: bfloat16 [768], P('head'), may hold values from -3 to 3
- value_bias_vector: bfloat16 [768], P('head'), may hold values from -3 to 3
- output_bias_vector: bfloat16 [768], replicated, may hold values from -3 to 3
- inner_bias_vector: bfloat16 [3072], P('head'), may hold values from -3 to 3
- outer_bias_vector: bfloat16 [768], replicated, may hold values from -3 to 3
- first_norm_scale: bfloat16 [768], replicated, may hold values from 0.099609375 to 1.8984375
- first_norm_bias: bfloat16 [768], replicated, may hold values from -2 to 2
- second_norm_scale: bfloat16 [768], replicated, may hold values from 0.099609375 to 1.8984375
- second_norm_bias: bfloat16 [768], replicated, may hold values from -2 to 2
- query_down_matrix: bfloat16 [768, 8], replicated, may hold values from -0.21875 to 0.21875
- value_down_matrix: bfloat16 [768, 8], replicated, may hold values from -0.21875 to 0.21875
- query_up_matrix: float32 [8, 768], P(None, 'head'), may hold values from -1.2 to 1.2
- value_up_matrix: float32 [8, 768], P(None, 'head'), may hold values from -1.2 to 1.2
- cotangent: bfloat16 [4, 8192, 768], P(None, 'dp'), may hold values from -6 to 6
Outputs:
- activations: bfloat16 [4, 8192, 768], P(None, 'dp')
- input_grad: bfloat16 [4, 8192, 768], P(None, 'dp')
- lora_query_grad: float32 [8, 768], P(None, 'head')
- lora_value_grad: float32 [8, 768], P(None, 'head')
Inputs may be any that keep to these rules, and one draw needn't show every extreme that they name: The four micro-batches take the bucket lengths 512, 256, 128 and 64, each once. The slots of micro-batch m form aligned items of bucket[m] slots; live is 1 on a prefix of each item longer than half of it and 0 after.
All inputs are finite; a program needn't handle non-finite values.
Results may differ from a plain program's by a relative error of at most 0.02.
Values may be sent and summed in bfloat16 or wider, within the bound.
No kernel may reach another device: no remote copies, remote signals or barrier semaphores. Data moves between devices by JAX's collectives and lax.ppermute only.
A program may use at most 192 MiB of HBM per device.

v0:
```python
import math
import jax
import jax.numpy as jnp
from jax import lax
from jax.sharding import PartitionSpec as P

HEAD_DIM = 64
ADAPTER_RANK = 8
ALPHA = 16
BUCKET_TOP = 512
eps_norm = 1e-05
masked_score = -1000000000.0
highest = lax.Precision.HIGHEST


def plain_dot(left, right):
    return jnp.dot(left, right, preferred_element_type=jnp.float32)


def back_dot(left, right):
    return lax.dot_general(
        left, right, (((1,), (1,)), ((), ())), preferred_element_type=jnp.float32
    )


def precise_backward(left, right):
    return lax.dot_general(
        left, right, (((1,), (1,)), ((), ())), precision=highest, preferred_element_type=jnp.float32
    )


def norm_rows(rows_in, gain, shift):
    center = rows_in - jnp.mean(rows_in, axis=-1, keepdims=True)
    spread = jnp.mean(center * center, axis=-1, keepdims=True)
    scaled = lax.rsqrt(spread + eps_norm)
    normalized_rows = center * scaled
    return (normalized_rows * gain + shift, normalized_rows, scaled)


def norm_back(grad_in, normalized_rows, scaled, gain):
    weighted = grad_in * gain
    return scaled * (
        weighted
        - jnp.mean(weighted, axis=-1, keepdims=True)
        - normalized_rows * jnp.mean(weighted * normalized_rows, axis=-1, keepdims=True)
    )


def gelu_slope(value_matrix):
    cdf_part = 0.5 * (1.0 + lax.erf(value_matrix / math.sqrt(2.0)))
    pdf_part = jnp.exp(-0.5 * value_matrix * value_matrix) / math.sqrt(2.0 * math.pi)
    return cdf_part + value_matrix * pdf_part


def collect(
    query_weight,
    key_weight,
    value_weight,
    inner_weight,
    output_weight,
    outer_weight,
    inner_bias_vector,
):
    rows_q, rows_k, rows_v, rows_in = (
        lax.all_gather(query_weight, "dp", axis=0, tiled=True),
        lax.all_gather(key_weight, "dp", axis=0, tiled=True),
        lax.all_gather(value_weight, "dp", axis=0, tiled=True),
        lax.all_gather(inner_weight, "dp", axis=0, tiled=True),
    )
    cols_out, cols_ffn = (
        lax.all_gather(output_weight, "dp", axis=1, tiled=True),
        lax.all_gather(outer_weight, "dp", axis=1, tiled=True),
    )
    return (
        rows_q,
        rows_k,
        rows_v,
        rows_in,
        cols_out,
        cols_ffn,
        inner_bias_vector.astype(jnp.float32),
    )


def adapter_gradient_sum(query_gradient, value_gradient):
    return lax.psum((query_gradient, value_gradient), "dp")


def shards(
    tokens,
    live,
    bucket,
    query_weight,
    key_weight,
    value_weight,
    output_weight,
    inner_weight,
    outer_weight,
    query_bias_vector,
    value_bias_vector,
    output_bias_vector,
    inner_bias_vector,
    outer_bias_vector,
    first_norm_scale,
    first_norm_bias,
    second_norm_scale,
    second_norm_bias,
    query_down_matrix,
    value_down_matrix,
    query_up_matrix,
    value_up_matrix,
    cotangent,
):
    micro_count, slots, model_width = tokens.shape
    width = query_weight.shape[1]
    group = width // HEAD_DIM
    blocks = slots // BUCKET_TOP
    adapter_multiplier = ALPHA / ADAPTER_RANK
    inverse = 1.0 / math.sqrt(HEAD_DIM)
    bias_q = query_bias_vector.astype(jnp.float32)
    bias_v = value_bias_vector.astype(jnp.float32)
    bias_out = output_bias_vector.astype(jnp.float32)
    bias_ffn = outer_bias_vector.astype(jnp.float32)
    gain_first = first_norm_scale.astype(jnp.float32)
    shift_first = first_norm_bias.astype(jnp.float32)
    gain_second = second_norm_scale.astype(jnp.float32)
    shift_second = second_norm_bias.astype(jnp.float32)
    down_q32 = query_down_matrix.astype(jnp.float32)
    down_v32 = value_down_matrix.astype(jnp.float32)
    query_total_sum = jnp.zeros(query_up_matrix.shape, jnp.float32)
    value_total_sum = jnp.zeros(value_up_matrix.shape, jnp.float32)
    positions = lax.iota(jnp.int32, BUCKET_TOP)
    outputs = []
    grads = []
    for section in range(micro_count):
        rows_q, rows_k, rows_v, rows_in, cols_out, cols_ffn, bias_in = collect(
            query_weight,
            key_weight,
            value_weight,
            inner_weight,
            output_weight,
            outer_weight,
            inner_bias_vector,
        )
        section_tokens = tokens[section]
        tokens_f32 = section_tokens.astype(jnp.float32)
        section_live = live[section]
        segment = positions // bucket[section]
        same_item = segment[:, None] == segment[None, :]
        live_keys = section_live.reshape(blocks, BUCKET_TOP) == 1
        permitted_mask = (same_item[None, :, :] & live_keys[:, None, :])[:, None, :, :]
        query_down_rows = plain_dot(section_tokens, query_down_matrix).astype(jnp.bfloat16)
        value_down_rows = plain_dot(section_tokens, value_down_matrix).astype(jnp.bfloat16)
        query_matrix = (
            plain_dot(section_tokens, rows_q)
            + bias_q
            + adapter_multiplier
            * jnp.dot(
                query_down_rows.astype(jnp.float32),
                query_up_matrix,
                precision=highest,
                preferred_element_type=jnp.float32,
            )
        )
        value_matrix = (
            plain_dot(section_tokens, rows_v)
            + bias_v
            + adapter_multiplier
            * jnp.dot(
                value_down_rows.astype(jnp.float32),
                value_up_matrix,
                precision=highest,
                preferred_element_type=jnp.float32,
            )
        )
        query_heads = query_matrix.astype(jnp.bfloat16).reshape(blocks, BUCKET_TOP, group, HEAD_DIM)
        key_heads = (
            plain_dot(section_tokens, rows_k)
            .astype(jnp.bfloat16)
            .reshape(blocks, BUCKET_TOP, group, HEAD_DIM)
        )
        value_heads = value_matrix.astype(jnp.bfloat16).reshape(blocks, BUCKET_TOP, group, HEAD_DIM)
        scores = (
            jnp.einsum(
                "nqhd,nkhd->nhqk", query_heads, key_heads, preferred_element_type=jnp.float32
            )
            * inverse
        )
        scores = jnp.where(permitted_mask, scores, masked_score)
        top_score = jnp.max(scores, axis=-1, keepdims=True)
        expo = jnp.exp(scores - top_score)
        probs = expo / jnp.sum(expo, axis=-1, keepdims=True)
        probs_low = probs.astype(jnp.bfloat16)
        context = jnp.einsum(
            "nhqk,nkhd->nqhd", probs_low, value_heads, preferred_element_type=jnp.float32
        )
        context_low = context.reshape(slots, width).astype(jnp.bfloat16)
        attended = lax.psum(plain_dot(context_low, cols_out).astype(jnp.bfloat16), "head").astype(
            jnp.float32
        )
        normed, normal_one, scaled_one = norm_rows(
            tokens_f32 + attended + bias_out, gain_first, shift_first
        )
        normed_low = normed.astype(jnp.bfloat16)
        pre_act = plain_dot(normed_low, rows_in) + bias_in
        activated = jax.nn.gelu(pre_act, approximate=False).astype(jnp.bfloat16)
        fed = lax.psum(plain_dot(activated, cols_ffn).astype(jnp.bfloat16), "head").astype(
            jnp.float32
        )
        out_float, normal_two, scaled_two = norm_rows(
            normed + fed + bias_ffn, gain_second, shift_second
        )
        outputs.append(out_float.astype(jnp.bfloat16))
        grad_out = cotangent[section].astype(jnp.float32) * section_live[:, None].astype(
            jnp.float32
        )
        grad_r_two = norm_back(grad_out, normal_two, scaled_two, gain_second)
        grad_act = back_dot(grad_r_two.astype(jnp.bfloat16), cols_ffn)
        grad_pre = (grad_act * gelu_slope(pre_act)).astype(jnp.bfloat16)
        grad_normed = grad_r_two + lax.psum(
            back_dot(grad_pre, rows_in).astype(jnp.bfloat16), "head"
        ).astype(jnp.float32)
        grad_r_one = norm_back(grad_normed, normal_one, scaled_one, gain_first)
        grad_one_low = grad_r_one.astype(jnp.bfloat16)
        grad_context = back_dot(grad_one_low, cols_out).astype(jnp.bfloat16)
        grad_context = grad_context.reshape(blocks, BUCKET_TOP, group, HEAD_DIM)
        grad_probs = jnp.einsum(
            "nqhd,nkhd->nhqk", grad_context, value_heads, preferred_element_type=jnp.float32
        )
        grad_value = jnp.einsum(
            "nhqk,nqhd->nkhd", probs_low, grad_context, preferred_element_type=jnp.float32
        )
        row_total = jnp.sum(probs * grad_probs, axis=-1, keepdims=True)
        grad_scores = (probs * (grad_probs - row_total)).astype(jnp.bfloat16)
        grad_query = (
            jnp.einsum(
                "nhqk,nkhd->nqhd", grad_scores, key_heads, preferred_element_type=jnp.float32
            )
            * inverse
        )
        grad_key = (
            jnp.einsum(
                "nhqk,nqhd->nkhd", grad_scores, query_heads, preferred_element_type=jnp.float32
            )
            * inverse
        )
        query_gradient_reduced = grad_query.reshape(slots, width).astype(jnp.bfloat16)
        grad_k_low = grad_key.reshape(slots, width).astype(jnp.bfloat16)
        value_gradient_reduced = grad_value.reshape(slots, width).astype(jnp.bfloat16)
        query_down_gradient = adapter_multiplier * precise_backward(
            query_gradient_reduced.astype(jnp.float32), query_up_matrix
        )
        value_down_gradient = adapter_multiplier * precise_backward(
            value_gradient_reduced.astype(jnp.float32), value_up_matrix
        )
        input_part = (
            back_dot(query_gradient_reduced, rows_q)
            + back_dot(grad_k_low, rows_k)
            + back_dot(value_gradient_reduced, rows_v)
        )
        input_part = (
            input_part
            + precise_backward(query_down_gradient, down_q32)
            + precise_backward(value_down_gradient, down_v32)
        )
        grad_tokens = grad_r_one + lax.psum(input_part.astype(jnp.bfloat16), "head").astype(
            jnp.float32
        )
        grads.append(grad_tokens.astype(jnp.bfloat16))
        query_adapter_term = adapter_multiplier * lax.dot_general(
            query_down_rows,
            query_gradient_reduced,
            (((0,), (0,)), ((), ())),
            preferred_element_type=jnp.float32,
        )
        value_adapter_term = adapter_multiplier * lax.dot_general(
            value_down_rows,
            value_gradient_reduced,
            (((0,), (0,)), ((), ())),
            preferred_element_type=jnp.float32,
        )
        query_summed_rows, value_summed_rows = adapter_gradient_sum(
            query_adapter_term, value_adapter_term
        )
        query_total_sum = query_total_sum + query_summed_rows
        value_total_sum = value_total_sum + value_summed_rows
    return (jnp.stack(outputs), jnp.stack(grads), query_total_sum, value_total_sum)


def solution(mesh):
    return jax.shard_map(
        shards,
        mesh=mesh,
        in_specs=(
            P(None, "dp", None),
            P(None, "dp"),
            P(),
            P("dp", "head"),
            P("dp", "head"),
            P("dp", "head"),
            P("head", "dp"),
            P("dp", "head"),
            P("head", "dp"),
            P("head"),
            P("head"),
            P(),
            P("head"),
            P(),
            P(),
            P(),
            P(),
            P(),
            P(),
            P(),
            P(None, "head"),
            P(None, "head"),
            P(None, "dp", None),
        ),
        out_specs=(P(None, "dp", None), P(None, "dp", None), P(None, "head"), P(None, "head")),
        check_vma=False,
    )
```

profile of v0, /device:TPU:0, one launch (start us, length us, event | category | flops | bytes accessed | tf_op | source)
XLA Modules:
  0.0 754.8 jit_solution(17762407008141377688)
XLA Ops:
  14.7 24.8 %all_gather.14 = bf16[768,384]{1,0:T(8,128)(2,1)S(1)} all-gather(bf16[48,384]{1,0:T(8,128)(2,1)S(1)} %copy-done.104), channel_id=1, replica_groups=mesh['dp'=16,'head'=2] {'dp'}, dimensions={0}, use_global_device_ids=true | all-gather | bytes 626688 | tf_op jit(solution)/shard_map/all_gather | solution.py:66
  42.1 19.1 %all_gather.12 = bf16[768,384]{1,0:T(8,128)(2,1)S(1)} all-gather(bf16[48,384]{1,0:T(8,128)(2,1)S(1)} %copy-done.105), channel_id=1, replica_groups=mesh['dp'=16,'head'=2] {'dp'}, dimensions={0}, use_global_device_ids=true | all-gather | bytes 626688 | tf_op jit(solution)/shard_map/all_gather | solution.py:67
  64.1 20.5 %all_gather.13 = bf16[768,384]{1,0:T(8,128)(2,1)S(1)} all-gather(bf16[48,384]{1,0:T(8,128)(2,1)S(1)} %copy-done.106), channel_id=1, replica_groups=mesh['dp'=16,'head'=2] {'dp'}, dimensions={0}, use_global_device_ids=true | all-gather | bytes 626688 | tf_op jit(solution)/shard_map/all_gather | solution.py:65
  94.9 20.9 %all_gather.15 = bf16[384,768]{0,1:T(8,128)(2,1)} all-gather(bf16[384,48]{0,1:T(8,128)(2,1)S(1)} %copy-done.107), channel_id=1, replica_groups=mesh['dp'=16,'head'=2] {'dp'}, dimensions={1}, use_global_device_ids=true | all-gather | bytes 626688 | tf_op jit(solution)/shard_map/all_gather | solution.py:71
  124.6 6.7 fusion.448
  137.7 6.7 fusion.447
  163.2 6.9 fusion.450
  175.3 24.6 %all-reduce.24.cloned.1.call-done = (bf16[512,768]{1,0:T(8,128)(2,1)}, bf16[512,768]{1,0:T(8,128)(2,1)}) async-done(((bf16[512,768]{1,0:T(8,128)(2,1)}, bf16[512,768]{1,0:T(8,128)(2,1)}), (bf16[512,768]{1,0:T(8,128)(2,1)}, bf16[512,768]{1,0:T(8,128)(2,1)})) %all-reduce.24.cloned.1.call-update) | async-done | bytes 1572880 | tf_op jit(solution)/shard_map/psum | solution.py:198
  212.9 24.3 %all-gather.5.cloned.1.call-done = bf16[1536,768]{0,1:T(8,128)(2,1)} async-done(((bf16[1536,48]{0,1:T(8,128)(2,1)}), bf16[1536,768]{0,1:T(8,128)(2,1)}) %all-gather.5.cloned.1.call-update) | async-done | bytes 2359312 | tf_op jit(solution)/shard_map/all_gather | solution.py:72
  237.3 11.2 %fusion.141 = bf16[512,768]{1,0:T(8,128)(2,1)} fusion(bf16[1536,768]{0,1:T(8,128)(2,1)} %all-gather.5.cloned.1.call-done, f32[512,1536]{1,0:T(8,128)} %convolution_add_fusion), kind=kOutput, calls=%fused_computation.257 | convolution fusion | flops 1259470848 | bytes 6291456 | tf_op jit(solution)/shard_map/dot_general | solution.py:17
  248.5 8.8 %fusion.132 = bf16[512,768]{1,0:T(8,128)(2,1)} fusion(bf16[1536,768]{0,1:T(8,128)(2,1)S(1)} %copy-done.159, f32[512,1536]{1,0:T(8,128)S(1)} %copy-done.161), kind=kOutput, calls=%fused_computation.254 | convolution fusion | flops 1259470848 | bytes 6291456 | tf_op jit(solution)/shard_map/dot_general | solution.py:17
  263.0 6.8 fusion.449
  275.0 32.6 %all-reduce.22.cloned.1.call-done = (bf16[512,768]{1,0:T(8,128)(2,1)}, bf16[512,768]{1,0:T(8,128)(2,1)}) async-done(((bf16[512,768]{1,0:T(8,128)(2,1)}, bf16[512,768]{1,0:T(8,128)(2,1)}), (bf16[512,768]{1,0:T(8,128)(2,1)}, bf16[512,768]{1,0:T(8,128)(2,1)})) %all-reduce.22.cloned.1.call-update) | async-done | bytes 1572880 | tf_op jit(solution)/shard_map/psum | solution.py:207
  317.0 7.4 convolution_convert_fusion.3
  324.4 7.4 convolution_convert_fusion
  332.0 86.3 %all-reduce.20.cloned.1.call-done = (bf16[512,768]{1,0:T(8,128)(2,1)}, bf16[512,768]{1,0:T(8,128)(2,1)}, bf16[512,768]{1,0:T(8,128)(2,1)}, bf16[512,768]{1,0:T(8,128)(2,1)}) async-done(((bf16[512,768]{1,0:T(8,128)(2,1)}, bf16[512,768]{1,0:T(8,128)(2,1)}, bf16[512,768]{1,0:T(8,128)(2,1)}, bf16[512,768]{1,0:T(8,128)(2,1)}), (bf16[512,768]{1,0:T(8,128)(2,1)}, bf16[512,768]{1,0:T(8,128)(2,1)}, ...) | async-done | bytes 3145744 | tf_op jit(solution)/shard_map/psum | solution.py:198
  426.1 8.8 %fusion.138 = bf16[512,768]{1,0:T(8,128)(2,1)} fusion(bf16[1536,768]{0,1:T(8,128)(2,1)S(1)} %copy-done.160, f32[512,1536]{1,0:T(8,128)S(1)} %convolution_add_fusion.1), kind=kOutput, calls=%fused_computation.256 | convolution fusion | flops 1259470848 | bytes 6291456 | tf_op jit(solution)/shard_map/dot_general | solution.py:17
  438.1 9.0 %fusion.135 = bf16[512,768]{1,0:T(8,128)(2,1)} fusion(bf16[1536,768]{0,1:T(8,128)(2,1)S(1)} %copy-done.160, f32[512,1536]{1,0:T(8,128)S(1)} %convolution_add_fusion.2), kind=kOutput, calls=%fused_computation.255 | convolution fusion | flops 1259470848 | bytes 6291456 | tf_op jit(solution)/shard_map/dot_general | solution.py:17
  447.2 51.8 %all-reduce.18.cloned.1.call-done = (bf16[512,768]{1,0:T(8,128)(2,1)}, bf16[512,768]{1,0:T(8,128)(2,1)}) async-done(((bf16[512,768]{1,0:T(8,128)(2,1)}, bf16[512,768]{1,0:T(8,128)(2,1)}), (bf16[512,768]{1,0:T(8,128)(2,1)}, bf16[512,768]{1,0:T(8,128)(2,1)})) %all-reduce.18.cloned.1.call-update) | async-done | bytes 1572880 | tf_op jit(solution)/shard_map/psum | solution.py:207
  508.3 7.4 convolution_convert_fusion.2
  515.7 7.4 convolution_convert_fusion.1
  524.3 50.6 %all-reduce.16.cloned.1.call-done = (bf16[512,768]{1,0:T(8,128)(2,1)}, bf16[512,768]{1,0:T(8,128)(2,1)}) async-done(((bf16[512,768]{1,0:T(8,128)(2,1)}, bf16[512,768]{1,0:T(8,128)(2,1)}), (bf16[512,768]{1,0:T(8,128)(2,1)}, bf16[512,768]{1,0:T(8,128)(2,1)})) %all-reduce.16.cloned.1.call-update) | async-done | bytes 1572880 | tf_op jit(solution)/shard_map/psum | solution.py:220
  661.5 61.2 %all-reduce = (f32[8,384]{1,0:T(8,128)}, f32[8,384]{1,0:T(8,128)}) all-reduce(f32[8,384]{1,0:T(8,128)S(1)} %fusion.201, f32[8,384]{1,0:T(8,128)S(1)} %fusion.200), channel_id=1, replica_groups=mesh['dp'=16,'head'=2] {'dp'}, use_global_device_ids=true, to_apply=%region_60.61 | all-reduce | flops 6144 | bytes 49152 | tf_op jit(solution)/shard_map/psum | solution.py:86
  722.7 18.7 %all-reduce.14.cloned.1.call-done = (bf16[512,768]{1,0:T(8,128)(2,1)}, bf16[512,768]{1,0:T(8,128)(2,1)}, bf16[512,768]{1,0:T(8,128)(2,1)}, bf16[512,768]{1,0:T(8,128)(2,1)}) async-done(((bf16[512,768]{1,0:T(8,128)(2,1)}, bf16[512,768]{1,0:T(8,128)(2,1)}, bf16[512,768]{1,0:T(8,128)(2,1)}, bf16[512,768]{1,0:T(8,128)(2,1)}), (bf16[512,768]{1,0:T(8,128)(2,1)}, bf16[512,768]{1,0:T(8,128)(2,1)}, ...) | async-done | bytes 3145744 | tf_op jit(solution)/shard_map/psum | solution.py:266
  (539 shorter events, 204.4 us)
Async XLA Ops:
  8.0 191.8 %all-reduce.24.cloned.1.call-start = ((), (), s32[]{:S(2)}) async-start(), calls=%async_computation.7 | async-start | bytes 3145728 | tf_op jit(solution)/shard_map/psum | solution.py:198
  9.7 111.0 %copy-start.111 = (bf16[512,8]{0,1:T(8,128)(2,1)}, bf16[512,8]{0,1:T(8,128)(2,1)S(1)}, u32[]{:S(2)}) copy-start(bf16[512,8]{0,1:T(8,128)(2,1)S(1)} %convolution_convert_fusion.16) | copy-start | bytes 24580
  13.2 102.6 %copy-start.113 = (bf16[512,8]{0,1:T(8,128)(2,1)}, bf16[512,8]{0,1:T(8,128)(2,1)S(1)}, u32[]{:S(2)}) copy-start(bf16[512,8]{0,1:T(8,128)(2,1)S(1)} %convolution_convert_fusion.17) | copy-start | bytes 24580
  14.7 103.6 %copy-start.109 = (bf16[512,8]{0,1:T(8,128)(2,1)}, bf16[512,8]{0,1:T(8,128)(2,1)S(1)}, u32[]{:S(2)}) copy-start(bf16[512,8]{0,1:T(8,128)(2,1)S(1)} %convolution_convert_fusion.23) | copy-start | bytes 24580
  42.1 43.8 %copy-start.149 = (f32[384]{0:T(512)}, f32[384]{0:T(512)S(1)}, u32[]{:S(2)}) copy-start(f32[384]{0:T(512)S(1)} %convert_element_type.605) | copy-start | bytes 4612
  64.1 51.8 %copy-start.76 = (f32[8,384]{1,0:T(8,128)S(1)}, f32[8,384]{1,0:T(8,128)}, u32[]{:S(2)}) copy-start(f32[8,384]{1,0:T(8,128)} %param.44) | copy-start | bytes 36868
  149.4 54.7 %all-gather.3.cloned.1.call-start = ((), (), s32[]{:S(2)}) async-start(), calls=%async_computation | async-start | bytes 2506752 | tf_op jit(solution)/shard_map/all_gather | solution.py:68
  150.0 87.2 %all-gather.5.cloned.1.call-start = ((), (), s32[]{:S(2)}) async-start(), calls=%async_computation.1 | async-start | bytes 2506752 | tf_op jit(solution)/shard_map/all_gather | solution.py:72
  150.6 157.0 %all-reduce.22.cloned.1.call-start = ((), (), s32[]{:S(2)}) async-start(), calls=%async_computation.6 | async-start | bytes 3145728 | tf_op jit(solution)/shard_map/psum | solution.py:207
  257.3 161.0 %all-reduce.20.cloned.1.call-start = ((), (), s32[]{:S(2)}) async-start(), calls=%async_computation.5 | async-start | bytes 6291456 | tf_op jit(solution)/shard_map/psum | solution.py:198
  269.8 37.8 %copy-start.98 = (f32[512]{0:T(512)S(1)}, f32[512]{0:T(512)}, u32[]{:S(2)}) copy-start(f32[512]{0:T(512)} %copy-done.97) | copy-start | bytes 6148
  269.8 37.8 %copy-start.102 = (f32[768]{0:T(1024)S(1)}, f32[768]{0:T(1024)}, u32[]{:S(2)}) copy-start(f32[768]{0:T(1024)} %convert_element_type.621) | copy-start | bytes 9220
  269.8 37.8 %copy-start.103 = (f32[768]{0:T(1024)S(1)}, f32[768]{0:T(1024)}, u32[]{:S(2)}) copy-start(f32[768]{0:T(1024)} %convert_element_type.627) | copy-start | bytes 9220
  269.9 37.8 %copy-start.125 = (f32[512]{0:T(512)S(1)}, f32[512]{0:T(512)}, u32[]{:S(2)}) copy-start(f32[512]{0:T(512)} %copy-done.124) | copy-start | bytes 6148
  269.9 37.8 %copy-start.128 = (f32[512]{0:T(512)S(1)}, f32[512]{0:T(512)}, u32[]{:S(2)}) copy-start(f32[512]{0:T(512)} %copy-done.127) | copy-start | bytes 6148
  331.8 167.2 %all-reduce.18.cloned.1.call-start = ((), (), s32[]{:S(2)}) async-start(), calls=%async_computation.4 | async-start | bytes 3145728 | tf_op jit(solution)/shard_map/psum | solution.py:207
  422.8 152.2 %copy-start.95 = (f32[512]{0:T(512)}, f32[512]{0:T(512)S(1)}, u32[]{:S(2)}) copy-start(f32[512]{0:T(512)S(1)} %broadcast_multiply_fusion.21) | copy-start | bytes 6148
  423.7 151.2 %copy-start.129 = (f32[512]{0:T(512)}, f32[512]{0:T(512)S(1)}, u32[]{:S(2)}) copy-start(f32[512]{0:T(512)S(1)} %add_rsqrt_fusion.5) | copy-start | bytes 6148
  447.2 127.7 %all-reduce.16.cloned.1.call-start = ((), (), s32[]{:S(2)}) async-start(), calls=%async_computation.3 | async-start | bytes 3145728 | tf_op jit(solution)/shard_map/psum | solution.py:220
  523.1 218.3 %all-reduce.14.cloned.1.call-start = ((), (), s32[]{:S(2)}) async-start(), calls=%async_computation.2 | async-start | bytes 6291456 | tf_op jit(solution)/shard_map/psum | solution.py:266
  584.3 64.1 %copy-start.45 = (bf16[6,64,512]{2,1,0:T(8,128)(2,1)}, bf16[6,64,512]{2,1,0:T(8,128)(2,1)S(1)}, u32[]{:S(2)}) copy-start(bf16[6,64,512]{2,1,0:T(8,128)(2,1)S(1)} %fusion.193) | copy-start | bytes 1179652
  597.9 52.1 %copy-start.47 = (bf16[6,64,512]{2,1,0:T(8,128)(2,1)}, bf16[6,64,512]{2,1,0:T(8,128)(2,1)S(1)}, u32[]{:S(2)}) copy-start(bf16[6,64,512]{2,1,0:T(8,128)(2,1)S(1)} %fusion.187) | copy-start | bytes 1179652
  613.7 37.8 %copy-start.49 = (bf16[6,64,512]{2,1,0:T(8,128)(2,1)}, bf16[6,64,512]{2,1,0:T(8,128)(2,1)S(1)}, u32[]{:S(2)}) copy-start(bf16[6,64,512]{2,1,0:T(8,128)(2,1)S(1)} %fusion.181) | copy-start | bytes 1179652
  659.4 81.9 %copy-start.30 = (f32[512,768]{1,0:T(8,128)S(1)}, f32[512,768]{1,0:T(8,128)}, u32[]{:S(2)}) copy-start(f32[512,768]{1,0:T(8,128)} %copy-done.29) | copy-start | bytes 4718596
  (156 other events, 1049.7 us)
Sparse Core Ops, SparseCore 0:
  149.6 50.2 all-reduce.23
  257.4 50.1 all-reduce.21
  331.9 86.3 all-reduce.19
  447.3 51.6 all-reduce.17
  523.2 51.6 all-reduce.15
  655.0 86.3 all-reduce.13
Sparse Core Ops, SparseCore 1:
  152.5 41.1 all-gather.2
  196.0 41.2 all-gather.4
where the time goes:
time: 760 us; the launch traced here: 755 us
  waiting for transfers between devices  290 us (38%)
  matrix products  215 us (28%)
  blocking collectives  146 us (19%)
  other arithmetic  73.9 us (10%)
  between operations  20.5 us (3%)
  local copies, waits for them, and re-layouts  8.15 us (1%)
    psum x2, waiting for transfers between devices, shards(): lax.psum(plain_dot(context_low, cols_out).astype(jnp.bfloat16), 'head')  111 us
    psum x2, waiting for transfers between devices, shards(): lax.psum(plain_dot(activated, cols_ffn).astype(jnp.bfloat16), 'head')  84.4 us
    dot_general x32, matrix products, plain_dot(): return jnp.dot(left, right, preferred_element_type=jnp.float32)  76.4 us
    psum x1, blocking collectives, adapter_gradient_sum(): return lax.psum((query_gradient, value_gradient), 'dp')  61.2 us
    psum x1, waiting for transfers between devices, shards(): lax.psum(back_dot(grad_pre, rows_in).astype(jnp.bfloat16), 'head')  50.6 us
    dot_general x20, matrix products, back_dot(): lax.dot_general(left, right, (((1,), (1,)), ((), ())), preferred_element_...  42.8 us
    sub x4, matrix products, shards(): expo = jnp.exp(scores - top_score)  27.1 us
    all_gather x1, blocking collectives, collect(): lax.all_gather(key_weight, 'dp', axis=0, tiled=True)  24.8 us
  transfers between devices with their start and end apart: 8, of which 7 were waited for; matrix products, arithmetic and copies ran while one was open for 8% of the time, Pallas kernels for 0%

commit v1 on v0

--- a/solution.py
+++ b/solution.py
@@ -11,6 +11,22 @@
 eps_norm = 1e-05
 masked_score = -1000000000.0
 highest = lax.Precision.HIGHEST
+
+
+def collect_2(x, axis, dim):
+    ways, here, step = (lax.axis_size(axis), lax.axis_index(axis), x.shape[dim])
+    shape = [n * ways if d == dim else n for d, n in enumerate(x.shape)]
+    full = lax.dynamic_update_slice_in_dim(jnp.zeros(shape, x.dtype), x, here * step, axis=dim)
+    going_up = going_down = x
+    for far in range(1, ways // 2 + 1):
+        going_up = lax.ppermute(going_up, axis, [(d, (d + 1) % ways) for d in range(ways)])
+        full = lax.dynamic_update_slice_in_dim(full, going_up, (here - far) % ways * step, axis=dim)
+        if 2 * far < ways:
+            going_down = lax.ppermute(going_down, axis, [(d, (d - 1) % ways) for d in range(ways)])
+            full = lax.dynamic_update_slice_in_dim(
+                full, going_down, (here + far) % ways * step, axis=dim
+            )
+    return full
 
 
 def plain_dot(left, right):
@@ -63,7 +79,7 @@
 ):
     rows_q, rows_k, rows_v, rows_in = (
         lax.all_gather(query_weight, "dp", axis=0, tiled=True),
-        lax.all_gather(key_weight, "dp", axis=0, tiled=True),
+        collect_2(key_weight, "dp", 0),
         lax.all_gather(value_weight, "dp", axis=0, tiled=True),
         lax.all_gather(inner_weight, "dp", axis=0, tiled=True),
     )

time: 760 us -> 813 us (1.070)
  starting transfers between devices: 1.08 us -> 34.1 us
  matrix products: 215 us -> 239 us
  blocking collectives: 146 us -> 123 us
  local copies, waits for them, and re-layouts: 8.15 us -> 25.2 us
    ppermute x0 -> x15, starting transfers between devices: none -> 32.6 us  [the longest x7 31.5 us: collect_2(): lax.ppermute(going_down, axis, [(d, (d - 1) % ways) for d in range(ways)])]
    all_gather x1 -> x0, blocking collectives: 24.8 us -> none  [collect(): lax.all_gather(key_weight, 'dp', axis=0, tiled=True)]
    dynamic_update_slice x0 -> x16, local copies, waits for them, and re-layouts: none -> 12.2 us  [the longest x8 5.67 us: collect_2(): lax.dynamic_update_slice_in_dim(full, going_up, (here - far) % ways * ste...]
    psum x2, waiting for transfers between devices: 111 us -> 102 us  [shards(): lax.psum(plain_dot(context_low, cols_out).astype(jnp.bfloat16), 'head')]
  transfers between devices with their start and end apart: 8 -> 23, of which waited for: 7 -> 15; matrix products, arithmetic and copies ran while one was open for 8% -> 13% of each run, Pallas kernels for 0% -> 0%
where the time goes in v1:
time: 813 us; the launch traced here: 806 us
  waiting for transfers between devices  291 us (36%)
  matrix products  239 us (29%)
  blocking collectives  123 us (15%)
  other arithmetic  73 us (9%)
  starting transfers between devices  34.1 us (4%)
  local copies, waits for them, and re-layouts  25.2 us (3%)
  between operations  20.4 us (3%)
    psum x2, waiting for transfers between devices, shards(): lax.psum(plain_dot(context_low, cols_out).astype(jnp.bfloat16), 'head')  102 us
    psum x2, waiting for transfers between devices, shards(): lax.psum(plain_dot(activated, cols_ffn).astype(jnp.bfloat16), 'head')  87.1 us
    dot_general x32, matrix products, plain_dot(): return jnp.dot(left, right, preferred_element_type=jnp.float32)  81.7 us
    psum x1, blocking collectives, adapter_gradient_sum(): return lax.psum((query_gradient, value_gradient), 'dp')  61.2 us
    psum x1, waiting for transfers between devices, shards(): lax.psum(back_dot(grad_pre, rows_in).astype(jnp.bfloat16), 'head')  51.7 us
    dot_general x20, matrix products, back_dot(): lax.dot_general(left, right, (((1,), (1,)), ((), ())), preferred_element_...  50.9 us
    ppermute x7, starting transfers between devices, collect_2(): lax.ppermute(going_down, axis, [(d, (d - 1) % ways) for d in range(ways)])  31.5 us
    sub x4, matrix products, shards(): expo = jnp.exp(scores - top_score)  27.2 us
  transfers between devices with their start and end apart: 23, of which 15 were waited for; matrix products, arithmetic and copies ran while one was open for 13% of the time, Pallas kernels for 0%

profile of v1, /device:TPU:0, one launch (start us, length us, event | category | flops | bytes accessed | tf_op | source)
XLA Modules:
  0.0 805.9 jit_solution(1265749187149874717)
XLA Ops:
  13.6 21.2 %all_gather.11 = bf16[768,384]{1,0:T(8,128)(2,1)S(1)} all-gather(bf16[48,384]{1,0:T(8,128)(2,1)} %param.26), channel_id=1, replica_groups=mesh['dp'=16,'head'=2] {'dp'}, dimensions={0}, use_global_device_ids=true | all-gather | bytes 626688 | tf_op jit(solution)/shard_map/all_gather | solution.py:81
  41.8 19.0 %all_gather.10 = bf16[768,384]{1,0:T(8,128)(2,1)S(1)} all-gather(bf16[48,384]{1,0:T(8,128)(2,1)S(1)} %copy-done.103), channel_id=1, replica_groups=mesh['dp'=16,'head'=2] {'dp'}, dimensions={0}, use_global_device_ids=true | all-gather | bytes 626688 | tf_op jit(solution)/shard_map/all_gather | solution.py:83
  68.1 21.8 %all_gather.12 = bf16[384,768]{0,1:T(8,128)(2,1)} all-gather(bf16[384,48]{0,1:T(8,128)(2,1)S(1)} %copy-done.104), channel_id=1, replica_groups=mesh['dp'=16,'head'=2] {'dp'}, dimensions={1}, use_global_device_ids=true | all-gather | bytes 626688 | tf_op jit(solution)/shard_map/all_gather | solution.py:87
  156.9 6.8 fusion.448
  168.7 6.7 fusion.447
  202.4 6.8 fusion.449
  214.0 15.6 %all-reduce.24.cloned.1.call-done = (bf16[512,768]{1,0:T(8,128)(2,1)}, bf16[512,768]{1,0:T(8,128)(2,1)}) async-done(((bf16[512,768]{1,0:T(8,128)(2,1)}, bf16[512,768]{1,0:T(8,128)(2,1)}), (bf16[512,768]{1,0:T(8,128)(2,1)}, bf16[512,768]{1,0:T(8,128)(2,1)})) %all-reduce.24.cloned.1.call-update) | async-done | bytes 1572880 | tf_op jit(solution)/shard_map/psum | solution.py:214
  242.7 24.4 %all-gather.5.cloned.1.call-done = bf16[1536,768]{0,1:T(8,128)(2,1)} async-done(((bf16[1536,48]{0,1:T(8,128)(2,1)}), bf16[1536,768]{0,1:T(8,128)(2,1)}) %all-gather.5.cloned.1.call-update) | async-done | bytes 2359312 | tf_op jit(solution)/shard_map/all_gather | solution.py:88
  267.1 11.2 %fusion.132 = bf16[512,768]{1,0:T(8,128)(2,1)} fusion(bf16[1536,768]{0,1:T(8,128)(2,1)} %all-gather.5.cloned.1.call-done, f32[512,1536]{1,0:T(8,128)} %convolution_add_fusion.3), kind=kOutput, calls=%fused_computation.254 | convolution fusion | flops 1259470848 | bytes 6291456 | tf_op jit(solution)/shard_map/dot_general | solution.py:33
  278.3 8.8 %fusion.141 = bf16[512,768]{1,0:T(8,128)(2,1)} fusion(bf16[1536,768]{0,1:T(8,128)(2,1)S(1)} %copy-done.154, f32[512,1536]{1,0:T(8,128)S(1)} %copy-done.156), kind=kOutput, calls=%fused_computation.257 | convolution fusion | flops 1259470848 | bytes 6291456 | tf_op jit(solution)/shard_map/dot_general | solution.py:33
  290.1 6.9 fusion.450
  302.2 35.3 %all-reduce.22.cloned.1.call-done = (bf16[512,768]{1,0:T(8,128)(2,1)}, bf16[512,768]{1,0:T(8,128)(2,1)}) async-done(((bf16[512,768]{1,0:T(8,128)(2,1)}, bf16[512,768]{1,0:T(8,128)(2,1)}), (bf16[512,768]{1,0:T(8,128)(2,1)}, bf16[512,768]{1,0:T(8,128)(2,1)})) %all-reduce.22.cloned.1.call-update) | async-done | bytes 1572880 | tf_op jit(solution)/shard_map/psum | solution.py:223
  346.9 7.4 convolution_convert_fusion
  354.3 7.4 convolution_convert_fusion.3
  362.1 86.0 %all-reduce.20.cloned.1.call-done = (bf16[512,768]{1,0:T(8,128)(2,1)}, bf16[512,768]{1,0:T(8,128)(2,1)}, bf16[512,768]{1,0:T(8,128)(2,1)}, bf16[512,768]{1,0:T(8,128)(2,1)}) async-done(((bf16[512,768]{1,0:T(8,128)(2,1)}, bf16[512,768]{1,0:T(8,128)(2,1)}, bf16[512,768]{1,0:T(8,128)(2,1)}, bf16[512,768]{1,0:T(8,128)(2,1)}), (bf16[512,768]{1,0:T(8,128)(2,1)}, bf16[512,768]{1,0:T(8,128)(2,1)}, ...) | async-done | bytes 3145744 | tf_op jit(solution)/shard_map/psum | solution.py:214
  456.0 8.8 %fusion.135 = bf16[512,768]{1,0:T(8,128)(2,1)} fusion(bf16[1536,768]{0,1:T(8,128)(2,1)S(1)} %copy-done.155, f32[512,1536]{1,0:T(8,128)S(1)} %convolution_add_fusion.2), kind=kOutput, calls=%fused_computation.255 | convolution fusion | flops 1259470848 | bytes 6291456 | tf_op jit(solution)/shard_map/dot_general | solution.py:33
  468.0 9.0 %fusion.138 = bf16[512,768]{1,0:T(8,128)(2,1)} fusion(bf16[1536,768]{0,1:T(8,128)(2,1)S(1)} %copy-done.155, f32[512,1536]{1,0:T(8,128)S(1)} %convolution_add_fusion.1), kind=kOutput, calls=%fused_computation.256 | convolution fusion | flops 1259470848 | bytes 6291456 | tf_op jit(solution)/shard_map/dot_general | solution.py:33
  477.1 51.8 %all-reduce.18.cloned.1.call-done = (bf16[512,768]{1,0:T(8,128)(2,1)}, bf16[512,768]{1,0:T(8,128)(2,1)}) async-done(((bf16[512,768]{1,0:T(8,128)(2,1)}, bf16[512,768]{1,0:T(8,128)(2,1)}), (bf16[512,768]{1,0:T(8,128)(2,1)}, bf16[512,768]{1,0:T(8,128)(2,1)})) %all-reduce.18.cloned.1.call-update) | async-done | bytes 1572880 | tf_op jit(solution)/shard_map/psum | solution.py:223
  538.1 7.4 convolution_convert_fusion.1
  545.5 7.4 convolution_convert_fusion.2
  553.0 51.7 %all-reduce.16.cloned.1.call-done = (bf16[512,768]{1,0:T(8,128)(2,1)}, bf16[512,768]{1,0:T(8,128)(2,1)}) async-done(((bf16[512,768]{1,0:T(8,128)(2,1)}, bf16[512,768]{1,0:T(8,128)(2,1)}), (bf16[512,768]{1,0:T(8,128)(2,1)}, bf16[512,768]{1,0:T(8,128)(2,1)})) %all-reduce.16.cloned.1.call-update) | async-done | bytes 1572880 | tf_op jit(solution)/shard_map/psum | solution.py:236
  653.3 6.6 multiply_convert_fusion.2
  713.1 61.2 %all-reduce = (f32[8,384]{1,0:T(8,128)}, f32[8,384]{1,0:T(8,128)}) all-reduce(f32[8,384]{1,0:T(8,128)S(1)} %fusion.201, f32[8,384]{1,0:T(8,128)S(1)} %fusion.200), channel_id=1, replica_groups=mesh['dp'=16,'head'=2] {'dp'}, use_global_device_ids=true, to_apply=%region_60.61 | all-reduce | flops 6144 | bytes 49152 | tf_op jit(solution)/shard_map/psum | solution.py:102
  774.3 18.6 %all-reduce.14.cloned.1.call-done = (bf16[512,768]{1,0:T(8,128)(2,1)}, bf16[512,768]{1,0:T(8,128)(2,1)}, bf16[512,768]{1,0:T(8,128)(2,1)}, bf16[512,768]{1,0:T(8,128)(2,1)}) async-done(((bf16[512,768]{1,0:T(8,128)(2,1)}, bf16[512,768]{1,0:T(8,128)(2,1)}, bf16[512,768]{1,0:T(8,128)(2,1)}, bf16[512,768]{1,0:T(8,128)(2,1)}), (bf16[512,768]{1,0:T(8,128)(2,1)}, bf16[512,768]{1,0:T(8,128)(2,1)}, ...) | async-done | bytes 3145744 | tf_op jit(solution)/shard_map/psum | solution.py:282
  (580 shorter events, 277.6 us)
Async XLA Ops:
  8.0 221.6 %all-reduce.24.cloned.1.call-start = ((), (), s32[]{:S(2)}) async-start(), calls=%async_computation.7 | async-start | bytes 3145728 | tf_op jit(solution)/shard_map/psum | solution.py:214
  8.1 99.5 %collective-permute-start = (bf16[48,384]{1,0:T(8,128)(2,1)}, bf16[48,384]{1,0:T(8,128)(2,1)}, u32[]{:S(2)}, u32[]{:S(2)}) collective-permute-start(bf16[48,384]{1,0:T(8,128)(2,1)} %param.27), channel_id=1, source_target_pairs={{0,2},{2,4},{4,6},{6,8},{8,10},{10,12},{12,14},{14,16},{16,18},{18... | collective-permute-start | bytes 110600 | tf_op jit(solution)/shard_map/ppermute | solution.py:22
  8.6 99.4 %collective-permute-start.1 = (bf16[48,384]{1,0:T(8,128)(2,1)}, bf16[48,384]{1,0:T(8,128)(2,1)}, u32[]{:S(2)}, u32[]{:S(2)}) collective-permute-start(bf16[48,384]{1,0:T(8,128)(2,1)} %param.27), channel_id=1, source_target_pairs={{0,30},{2,0},{4,2},{6,4},{8,6},{10,8},{12,10},{14,12},{16,14},{18,... | collective-permute-start | bytes 110600 | tf_op jit(solution)/shard_map/ppermute | solution.py:25
  107.6 7.2 collective-permute-start.2
  108.0 6.9 collective-permute-start.3
  114.8 6.1 collective-permute-start.4
  114.8 6.1 collective-permute-start.5
  120.9 6.1 collective-permute-start.6
  120.9 6.1 collective-permute-start.7
  127.0 6.1 collective-permute-start.8
  127.0 6.1 collective-permute-start.9
  133.1 6.1 collective-permute-start.10
  133.1 6.1 collective-permute-start.11
  139.2 6.1 collective-permute-start.12
  139.2 6.9 collective-permute-start.13
  145.2 6.4 collective-permute-start.14
  180.6 53.4 %all-gather.3.cloned.1.call-start = ((), (), s32[]{:S(2)}) async-start(), calls=%async_computation | async-start | bytes 2506752 | tf_op jit(solution)/shard_map/all_gather | solution.py:84
  181.1 86.0 %all-gather.5.cloned.1.call-start = ((), (), s32[]{:S(2)}) async-start(), calls=%async_computation.1 | async-start | bytes 2506752 | tf_op jit(solution)/shard_map/all_gather | solution.py:88
  181.7 155.8 %all-reduce.22.cloned.1.call-start = ((), (), s32[]{:S(2)}) async-start(), calls=%async_computation.6 | async-start | bytes 3145728 | tf_op jit(solution)/shard_map/psum | solution.py:223
  287.2 161.0 %all-reduce.20.cloned.1.call-start = ((), (), s32[]{:S(2)}) async-start(), calls=%async_computation.5 | async-start | bytes 6291456 | tf_op jit(solution)/shard_map/psum | solution.py:214
  361.7 167.1 %all-reduce.18.cloned.1.call-start = ((), (), s32[]{:S(2)}) async-start(), calls=%async_computation.4 | async-start | bytes 3145728 | tf_op jit(solution)/shard_map/psum | solution.py:223
  477.0 127.8 %all-reduce.16.cloned.1.call-start = ((), (), s32[]{:S(2)}) async-start(), calls=%async_computation.3 | async-start | bytes 3145728 | tf_op jit(solution)/shard_map/psum | solution.py:236
  552.9 240.0 %all-reduce.14.cloned.1.call-start = ((), (), s32[]{:S(2)}) async-start(), calls=%async_computation.2 | async-start | bytes 6291456 | tf_op jit(solution)/shard_map/psum | solution.py:282
  711.3 83.1 %copy-start.21 = (f32[512,768]{1,0:T(8,128)S(1)}, f32[512,768]{1,0:T(8,128)}, u32[]{:S(2)}) copy-start(f32[512,768]{1,0:T(8,128)} %copy-done.20) | copy-start | bytes 4718596
  (168 other events, 1347.4 us)
Sparse Core Ops, SparseCore 0:
  180.7 48.9 all-reduce.23
  287.3 50.1 all-reduce.21
  361.8 86.3 all-reduce.19
  477.1 51.6 all-reduce.17
  553.1 51.6 all-reduce.15
  706.5 86.3 all-reduce.13
Sparse Core Ops, SparseCore 1:
  183.6 39.8 all-gather.2
  225.9 41.2 all-gather.4
